TPU v7x, 32 devices: a whole 2x2x4 slice. The times are simulated.
32 devices in a mesh: ctx: 8 (over z, x), exp: 4 (over y, core).
Axes of the slice: x: 2, y: 2, z: 4, core: 2. Of those that a mesh axis runs over, the one named last changes fastest.
Arguments:
- residual: bfloat16 [4, 1024, 2048], P('exp', 'ctx'), may hold values from -54 to 54
- queries: bfloat16 [4, 1024, 2048], P('exp', 'ctx'), may hold values from -160 to 160
- key_states: bfloat16 [4, 1024, 256], P('exp', 'ctx'), may hold values from -6.1 to 6.1
- value_states: bfloat16 [4, 1024, 256], P('exp', 'ctx'), may hold values from -6 to 6
- expert_ids: int32 [4, 1024, 1], P('exp', 'ctx'), may hold values from 0 to 7; in each aligned block of 128 rows (0 to 127, 128 to 255, ..., all dimensions but the last counted through in order) at most 32 rows name the same one
- route_weight: float32 [4, 1024, 1], P('exp', 'ctx'), may hold values from 0.2 to 1
- gate_weight: bfloat16 [4, 8, 192, 2048], P('exp', 'ctx'), may hold values from -0.125 to 0.125
- up_weight: bfloat16 [4, 8, 192, 2048], P('exp', 'ctx'), may hold values from -0.125 to 0.125
- down_weight: bfloat16 [4, 8, 192, 2048], P('exp', 'ctx'), may hold values from -0.21875 to 0.21875
Outputs:
- output: bfloat16 [4, 1024, 2048], P('exp', 'ctx')
Inputs may be any that keep to these rules, and one draw needn't show every extreme that they name: `expert_ids`: within each aligned block of 128 rows (sequence by sequence, positions in order), which is the rows of one device, no expert is named more than 32 times, a bound that some block reaches; every expert is named somewhere.
All inputs are finite; a program needn't handle non-finite values.
Results may differ from a plain program's by a relative error of at most 0.003.
Values may be sent and summed in bfloat16 or wider, within the bound.
No kernel may reach another device: no remote copies, remote signals or barrier semaphores. Data moves between devices by JAX's collectives and lax.ppermute only.
A program may use at most 64 MiB of HBM per device.

v0:
```python
from functools import partial
import math
import jax
import jax.numpy as jnp
from jax import lax
from jax.sharding import PartitionSpec as P

HD = 128
HEADS = 16
KV_HEADS = 2
PIECES = 4
TOPK = 1
negative_fill = -1e30
epsilon = 1e-06


def contract_rows(left_rows, weight_rows):
    return lax.dot_general(
        left_rows, weight_rows, (((1,), (1,)), ((), ())), preferred_element_type=jnp.float32
    )


def to_groups(half_block, heads_kv, group_size, head_dim):
    token_count = half_block.shape[0]
    shaped = half_block.reshape(token_count, heads_kv, group_size, head_dim)
    return jnp.transpose(shaped, (1, 0, 2, 3)).reshape(heads_kv, token_count * group_size, head_dim)


def keep_current(current):
    return current


def block_update(current, query_rows, query_pos, key_block, value_block, key_start, score_scale):
    running_max, running_total, accumulated = current
    scores = (
        jnp.einsum("gqd,kgd->gqk", query_rows, key_block, preferred_element_type=jnp.float32)
        * score_scale
    )
    key_pos = key_start + jnp.arange(key_block.shape[0], dtype=jnp.int32)
    allowed = key_pos[None, None, :] <= query_pos[None, :, None]
    scores = jnp.where(allowed, scores, negative_fill)
    new_max = jnp.maximum(running_max, jnp.max(scores, axis=-1))
    rescale = jnp.exp(running_max - new_max)
    exponent = jnp.where(allowed, jnp.exp(scores - new_max[..., None]), 0.0)
    new_total = running_total * rescale + jnp.sum(exponent, axis=-1)
    product = jnp.einsum(
        "gqk,kgd->gqd",
        exponent.astype(jnp.bfloat16),
        value_block,
        preferred_element_type=jnp.float32,
    )
    return (new_max, new_total, accumulated * rescale[..., None] + product)


def make_folder(query_sets, position_sets, last_positions, heads_kv, head_dim, score_scale):

    def fold_keys(running, key_piece, first_key):
        key_part, value_part = key_piece
        key_count = key_part.shape[1]
        key_width = math.gcd(key_count, 512)
        key_rows = key_part.reshape(key_count, heads_kv, head_dim)
        value_rows = value_part.reshape(key_count, heads_kv, head_dim)

        def one_block(block_index, current_sets):
            offset = block_index * key_width
            key_block = lax.dynamic_slice_in_dim(key_rows, offset, key_width, 0)
            value_block = lax.dynamic_slice_in_dim(value_rows, offset, key_width, 0)
            updated = []
            for current, query_rows, query_pos, last_pos in zip(
                current_sets, query_sets, position_sets, last_positions
            ):
                step_fn = partial(
                    block_update,
                    query_rows=query_rows,
                    query_pos=query_pos,
                    key_block=key_block,
                    value_block=value_block,
                    key_start=offset,
                    score_scale=score_scale,
                )
                updated.append(lax.cond(offset <= last_pos, step_fn, keep_current, current))
            return tuple(updated)

        return lax.fori_loop(0, key_count // key_width, one_block, running)

    return fold_keys


def finish(current, token_count, heads_kv, group_size, head_dim):
    running_max, running_total, accumulated = current
    result = accumulated / running_total[..., None]
    shaped = result.reshape(heads_kv, token_count, group_size, head_dim)
    return (
        jnp.transpose(shaped, (1, 0, 2, 3))
        .reshape(token_count, heads_kv * group_size * head_dim)
        .astype(jnp.bfloat16)
    )


def shards(
    residual,
    queries,
    key_states,
    value_states,
    expert_ids,
    route_weight,
    gate_weight,
    up_weight,
    down_weight,
):
    ctx_count = lax.axis_size("ctx")
    exp_count = lax.axis_size("exp")
    ctx_rank = lax.axis_index("ctx")
    tok_rows = residual.shape[1]
    half_rows = tok_rows // 2
    group_size = HEADS // KV_HEADS
    score_scale = 1.0 / math.sqrt(HD)
    local_queries = queries[0]
    first_half = local_queries[:half_rows]
    second_half = local_queries[half_rows:]
    first_start = ctx_rank * tok_rows
    second_start = first_start + half_rows
    offsets = jnp.repeat(jnp.arange(half_rows, dtype=jnp.int32), group_size)
    query_sets = (
        to_groups(first_half, KV_HEADS, group_size, HD),
        to_groups(second_half, KV_HEADS, group_size, HD),
    )
    position_sets = (first_start + offsets, second_start + offsets)
    last_positions = (first_start + half_rows - 1, second_start + half_rows - 1)
    row_total = half_rows * group_size
    empty_state = (
        jnp.full((KV_HEADS, row_total), negative_fill, jnp.float32),
        jnp.zeros((KV_HEADS, row_total), jnp.float32),
        jnp.zeros((KV_HEADS, row_total, HD), jnp.float32),
    )
    folder = make_folder(query_sets, position_sets, last_positions, KV_HEADS, HD, score_scale)
    final_sets = folder(
        (empty_state, empty_state),
        (
            lax.all_gather(key_states, "ctx", axis=1, tiled=True),
            lax.all_gather(value_states, "ctx", axis=1, tiled=True),
        ),
        jnp.int32(0),
    )
    first_out = finish(final_sets[0], half_rows, KV_HEADS, group_size, HD)
    second_out = finish(final_sets[1], half_rows, KV_HEADS, group_size, HD)
    attention = jnp.concatenate([first_out, second_out], axis=0)
    summed = residual[0].astype(jnp.float32) + lax.optimization_barrier(attention).astype(
        jnp.float32
    )
    normed = (
        summed * lax.rsqrt(jnp.mean(summed * summed, axis=-1, keepdims=True) + epsilon)
    ).astype(jnp.bfloat16)
    width_model = normed.shape[1]
    experts_each = ctx_count // PIECES
    expert_total = experts_each * exp_count
    pair_count = tok_rows * TOPK
    capacity = max(2, 2 * tok_rows * TOPK // expert_total)
    flat_ids = expert_ids[0].reshape(pair_count)
    onehot = (flat_ids[:, None] == jnp.arange(expert_total, dtype=jnp.int32)[None, :]).astype(
        jnp.int32
    )
    earlier = jnp.cumsum(onehot, axis=0) - onehot
    slot_index = jnp.sum(earlier * onehot, axis=1)
    owner_index = flat_ids // experts_each
    local_expert = flat_ids % experts_each
    target = (local_expert * exp_count + owner_index) * capacity + slot_index
    pair_token = jnp.arange(pair_count, dtype=jnp.int32) // TOPK
    slot_total = expert_total * capacity
    slot_table = jnp.full((slot_total,), tok_rows, jnp.int32).at[target].set(pair_token)
    padded = jnp.concatenate([normed, jnp.zeros((1, width_model), jnp.bfloat16)], axis=0)
    outgoing = padded[slot_table].reshape(experts_each, exp_count, capacity, width_model)
    arrived = lax.all_to_all(outgoing, "exp", split_axis=1, concat_axis=1, tiled=True)
    copies = jnp.broadcast_to(
        arrived[:, None], (experts_each, PIECES, exp_count, capacity, width_model)
    ).reshape(ctx_count, exp_count * capacity, width_model)
    gate_piece = gate_weight[0, 0]
    up_piece = up_weight[0, 0]
    down_piece = down_weight[0, 0]
    received = lax.all_to_all(copies, "ctx", split_axis=0, concat_axis=0, tiled=True)
    sources = received.shape[0]
    item_count = received.shape[1]
    flat_rows = received.reshape(sources * item_count, width_model)
    gate_part = contract_rows(flat_rows, gate_piece)
    up_part = contract_rows(flat_rows, up_piece)
    active = (jax.nn.silu(gate_part) * up_part).astype(jnp.bfloat16)
    partial_out = jnp.dot(active, down_piece, preferred_element_type=jnp.float32).astype(
        jnp.bfloat16
    )
    returned = lax.all_to_all(
        partial_out.reshape(sources, item_count, width_model),
        "ctx",
        split_axis=0,
        concat_axis=0,
        tiled=True,
    )
    piece_sum = jnp.sum(
        returned.reshape(experts_each, PIECES, exp_count, capacity, width_model).astype(
            jnp.float32
        ),
        axis=1,
    ).astype(jnp.bfloat16)
    arrived_back = lax.all_to_all(piece_sum, "exp", split_axis=1, concat_axis=1, tiled=True)
    gathered = arrived_back.reshape(slot_total, width_model)[target].astype(jnp.float32)
    weighted = gathered * route_weight[0]
    mixture = jnp.sum(weighted.reshape(tok_rows, TOPK, width_model), axis=1)
    return (summed + mixture).astype(jnp.bfloat16)[None]


def solution(mesh):
    in_specs = (
        P("exp", "ctx", None),
        P("exp", "ctx", None),
        P("exp", "ctx", None),
        P("exp", "ctx", None),
        P("exp", "ctx", None),
        P("exp", "ctx", None),
        P("exp", "ctx", None, None),
        P("exp", "ctx", None, None),
        P("exp", "ctx", None, None),
    )
    out_specs = P("exp", "ctx", None)
    return jax.shard_map(shards, mesh=mesh, in_specs=in_specs, out_specs=out_specs, check_vma=False)
```

profile of v0, /device:TPU:0, one launch (start us, length us, event | category | flops | bytes accessed | tf_op | source)
XLA Modules:
  0.0 328.2 jit_solution(8292580245410848761)
XLA Ops:
  0.0 1.1 slice_bitcast_fusion
  1.4 29.6 %all_gather.6 = bf16[1,1024,256]{1,2,0:T(8,128)(2,1)S(1)} all-gather(bf16[1,128,256]{1,2,0:T(8,128)(2,1)S(1)} %copy.41), channel_id=1, replica_groups=mesh['ctx'=8,'exp'=4] {'ctx'}, dimensions={1}, use_global_device_ids=true | all-gather | bytes 589824 | tf_op jit(solution)/shard_map/all_gather | solution.py:140
  31.1 27.8 %all_gather.7 = bf16[1,1024,256]{1,2,0:T(8,128)(2,1)S(1)} all-gather(bf16[1,128,256]{1,2,0:T(8,128)(2,1)S(1)} %copy.42), channel_id=1, replica_groups=mesh['ctx'=8,'exp'=4] {'ctx'}, dimensions={1}, use_global_device_ids=true | all-gather | bytes 589824 | tf_op jit(solution)/shard_map/all_gather | solution.py:141
  59.0 0.8 broadcast_in_dim.78
  59.8 0.8 broadcast_in_dim.78.clone
  60.6 9.5 %while.24 = (s32[]{:T(128)}, f32[2,512]{1,0:T(2,128)S(1)}, f32[2,512]{1,0:T(2,128)S(1)}, f32[2,512,128]{2,1,0:T(8,128)}, f32[2,512]{1,0:T(2,128)S(1)}, /*index=5...) while((s32[]{:T(128)}, f32[2,512]{1,0:T(2,128)S(1)}, ...), condition=%wide.region_9.10_spmd.clone, body=%wide.region_0.9_spmd.clone.sunk | while | flops 551557120 | bytes 29000316 | solution.py:84
  61.1 3.4 %conditional.7 = ((f32[2,512]{1,0:T(2,128)S(1)}, f32[2,512]{1,0:T(2,128)S(1)}, f32[2,512,128]{2,1,0:T(8,128)})) conditional(s32[]{:T(128)} %convert_element_type.131, (f32[2,512]{1,0:T(2,128)S(1)}, f32[2,512]{1,0:T(2,128)S(1)}, f32[2,512,128]{2,1,0:T(8,128)}) %tuple.67, (s32[]{:T(128)}, s32[]{:T(128)}, bf16[2,512,128]{2,1,0:T(8,128)(2,1)S(1)}, ...), branch_computations={%region_5.5_spmd, %region_6.8_spmd} | conditional | flops 275778560 | bytes 13449312 | solution.py:81
  62.0 0.6 fusion.17
  62.6 1.1 convolution_add_fusion.1
  63.7 0.8 copy-done.6
  64.5 2.6 conditional.6
  65.4 0.6 fusion.6
  66.0 1.1 convolution_add_fusion
  67.1 0.8 copy-done.4
  68.4 1.0 copy-done.3
  69.4 0.8 copy-done.4
  70.2 1.3 fusion.39
  73.5 1.0 scatter_custom_fusion
  74.5 1.4 gather_fusion
  76.0 17.1 %all_to_all.20 = bf16[2,4,32,2048]{3,2,0,1:T(8,128)(2,1)S(1)} all-to-all(bf16[2,4,32,2048]{3,2,0,1:T(8,128)(2,1)S(1)} %copy.49), channel_id=1, replica_groups=mesh['ctx'=8,'exp'=4] {'exp'}, dimensions={1} | all-to-all | bytes 2097152 | tf_op jit(solution)/shard_map/all_to_all | solution.py:173
  93.7 99.7 %all_to_all.21 = bf16[8,128,2048]{2,1,0:T(8,128)(2,1)S(1)} all-to-all(bf16[8,128,2048]{2,1,0:T(8,128)(2,1)S(1)} %bitcast.91), channel_id=1, replica_groups=mesh['ctx'=8,'exp'=4] {'ctx'}, dimensions={0} | all-to-all | bytes 8388608 | tf_op jit(solution)/shard_map/all_to_all | solution.py:180
  193.4 2.0 copy-done.2
  195.4 2.5 fusion.30
  197.9 7.1 %convolution_convert_fusion = bf16[1024,2048]{1,0:T(8,128)(2,1)} fusion(bf16[1024,2048]{1,0:T(8,128)(2,1)} %bitcast.97, bf16[1,1,192,2048]{3,2,1,0:T(8,128)(2,1)S(1)} %copy-done, bf16[1,1,192,2048]{3,2,1,0:T(8,128)(2,1)S(1)} %copy-done.13, f32[1024,192]{0,1:T(8,128)} %fusion.30), kind=kOutput, calls=%fused_computation.43 | convolution fusion | flops 1613889536 | bytes 10747904 | tf_op jit(solution)/shard_map/dot_general | solution.py:187
  205.0 97.0 %all_to_all.22 = bf16[8,128,2048]{2,1,0:T(8,128)(2,1)} all-to-all(bf16[8,128,2048]{2,1,0:T(8,128)(2,1)} %bitcast.98), channel_id=1, replica_groups=mesh['ctx'=8,'exp'=4] {'ctx'}, dimensions={0} | all-to-all | bytes 8388608 | tf_op jit(solution)/shard_map/all_to_all | solution.py:190
  302.0 3.1 reduce_sum.57
  305.0 1.1 copy.51
  306.1 4.2 %all-to-all-start.3 = ((bf16[2,4,32,2048]{3,2,0,1:T(8,128)(2,1)}), bf16[2,4,32,2048]{3,2,0,1:T(8,128)(2,1)}, u32[]{:S(2)}, u32[]{:S(2)}) async-start(bf16[2,4,32,2048]{3,2,0,1:T(8,128)(2,1)} %copy.51), calls=%async_computation.3 | async-start | bytes 2097152 | tf_op jit(solution)/shard_map/all_to_all | solution.py:203
  310.4 14.5 %all-to-all-done.3 = bf16[2,4,32,2048]{3,2,0,1:T(8,128)(2,1)} async-done(((bf16[2,4,32,2048]{3,2,0,1:T(8,128)(2,1)}), bf16[2,4,32,2048]{3,2,0,1:T(8,128)(2,1)}, u32[]{:S(2)}, u32[]{:S(2)}) %all-to-all-start.3) | async-done | bytes 1048608 | tf_op jit(solution)/shard_map/all_to_all | solution.py:203
  324.9 1.3 copy.52
  326.2 0.9 gather_fusion.1
  327.1 1.1 fusion.37
  (85 shorter events, 5.6 us)
Async XLA Ops:
  0.0 197.9 %copy-start = (bf16[1,1,192,2048]{3,2,1,0:T(8,128)(2,1)S(1)}, bf16[1,1,192,2048]{3,2,1,0:T(8,128)(2,1)}, u32[]{:S(2)}) copy-start(bf16[1,1,192,2048]{3,2,1,0:T(8,128)(2,1)} %param.23) | copy-start | bytes 2359300
  0.0 1.3 copy-start.8
  0.0 30.9 %copy-start.9 = (bf16[1,128,256]{2,1,0:T(8,128)(2,1)S(1)}, bf16[1,128,256]{2,1,0:T(8,128)(2,1)}, u32[]{:S(2)}) copy-start(bf16[1,128,256]{2,1,0:T(8,128)(2,1)} %param.18) | copy-start | bytes 196612
  61.1 3.4 %copy-start.3 = (f32[2,512,128]{2,1,0:T(8,128)S(1)}, f32[2,512,128]{2,1,0:T(8,128)}, u32[]{:S(2)}) copy-start(f32[2,512,128]{2,1,0:T(8,128)} %get-tuple-element.613) | copy-start | bytes 1572868 | tf_op jit(solution)/shard_map/while
  61.5 1.2 copy-start.5
  63.7 0.8 copy-start.6
  67.1 0.8 copy-start.4
  68.3 1.0 copy-start.3
  69.4 0.8 copy-start.4
  70.2 1.5 copy-start.7
  71.5 1.0 copy-start.1
  71.9 1.1 copy-start.10
  93.7 101.7 %copy-start.12 = (bf16[1,1,192,2048]{3,2,1,0:T(8,128)(2,1)S(1)}, bf16[1,1,192,2048]{3,2,1,0:T(8,128)(2,1)}, u32[]{:S(2)}) copy-start(bf16[1,1,192,2048]{3,2,1,0:T(8,128)(2,1)} %param.21) | copy-start | bytes 2359300
  193.4 2.0 copy-start.2
  195.4 2.5 copy-start.13
  306.1 18.8 %all-to-all-start.3 = ((bf16[2,4,32,2048]{3,2,0,1:T(8,128)(2,1)}), bf16[2,4,32,2048]{3,2,0,1:T(8,128)(2,1)}, u32[]{:S(2)}, u32[]{:S(2)}) async-start(bf16[2,4,32,2048]{3,2,0,1:T(8,128)(2,1)} %copy.51), calls=%async_computation.3 | async-start | bytes 2097152 | tf_op jit(solution)/shard_map/all_to_all | solution.py:203
  326.2 1.0 copy-start.11
where the time goes:
time: 329 us; the launch traced here: 328 us
  blocking collectives  271 us (82%)
  local copies, waits for them, and re-layouts  16.7 us (5%)
  waiting for transfers between devices  14.5 us (4%)
  matrix products  12.8 us (4%)
  other arithmetic  8.21 us (2%)
  starting transfers between devices  4.23 us (1%)
    all_to_all x1, blocking collectives, shards(): lax.all_to_all(copies, 'ctx', split_axis=0, concat_axis=0, tiled=True)  99.7 us
    all_to_all x1, blocking collectives, shards(): lax.all_to_all(partial_out.reshape(sources, item_count, width_model), 'ct...  97 us
    all_gather x1, blocking collectives, shards(): lax.all_gather(key_states, 'ctx', axis=1, tiled=True)  29.6 us
    all_gather x1, blocking collectives, shards(): lax.all_gather(value_states, 'ctx', axis=1, tiled=True)  27.8 us
    all_to_all x1, blocking collectives, shards(): lax.all_to_all(outgoing, 'exp', split_axis=1, concat_axis=1, tiled=True)  17.1 us
    all_to_all x1, waiting for transfers between devices, shards(): lax.all_to_all(piece_sum, 'exp', split_axis=1, concat_axis=1, tiled=True)  14.5 us
    dot_general x1, matrix products, shards(): jnp.dot(active, down_piece, preferred_element_type=jnp.float32)  7.06 us
  transfers between devices with their start and end apart: 1, of which 1 were waited for; matrix products, arithmetic and copies ran while one was open for 0% of the time, Pallas kernels for 0%

commit v1 on v0

--- a/solution.py
+++ b/solution.py
@@ -12,6 +12,17 @@
 TOPK = 1
 negative_fill = -1e30
 epsilon = 1e-06
+
+
+def in_blocks(shard, dim, length):
+    before, after = (shard.shape[:dim], shard.shape[dim + 1 :])
+    return jnp.moveaxis(shard.reshape(*before, length, -1, *after), dim, 0)
+
+
+def in_order(pieces, dim):
+    shape = list(pieces.shape[1:])
+    shape[dim] *= pieces.shape[0]
+    return jnp.moveaxis(pieces, 0, dim).reshape(shape)
 
 
 def contract_rows(left_rows, weight_rows):
@@ -200,7 +211,15 @@
         ),
         axis=1,
     ).astype(jnp.bfloat16)
-    arrived_back = lax.all_to_all(piece_sum, "exp", split_axis=1, concat_axis=1, tiled=True)
+    length, index = (lax.axis_size("exp"), lax.axis_index("exp"))
+    tiles = in_blocks(piece_sum, 1, length)
+    out = tiles
+    for step in range(1, length):
+        target_2, source = ((index + step) % length, (index - step) % length)
+        sent = lax.dynamic_index_in_dim(tiles, target_2, 0)
+        other = lax.ppermute(sent, "exp", [(i, (i + step) % length) for i in range(length)])
+        out = lax.dynamic_update_slice_in_dim(out, other, source, axis=0)
+    arrived_back = in_order(out, 1)
     gathered = arrived_back.reshape(slot_total, width_model)[target].astype(jnp.float32)
     weighted = gathered * route_weight[0]
     mixture = jnp.sum(weighted.reshape(tok_rows, TOPK, width_model), axis=1)

time: 329 us -> 325 us (0.988)
  blocking collectives: 271 us -> 174 us
  waiting for transfers between devices: 14.5 us -> 101 us
    all_to_all x1 -> x0, blocking collectives: 97 us -> none  [shards(): lax.all_to_all(partial_out.reshape(sources, item_count, width_model), 'ct...]
    all_to_all x1, waiting for transfers between devices: 14.5 us -> 92.2 us  [shards(): lax.all_to_all(partial_out.reshape(sources, item_count, width_model), 'ct...]
    ppermute x0 -> x3, waiting for transfers between devices: none -> 8.52 us  [shards(): lax.ppermute(sent, 'exp', [(i, (i + step) % length) for i in range(length)])]
  transfers between devices with their start and end apart: 1 -> 4, of which waited for: 1 -> 3; matrix products, arithmetic and copies ran while one was open for 0% -> 1% of each run, Pallas kernels for 0% -> 0%
where the time goes in v1:
time: 325 us; the launch traced here: 322 us
  blocking collectives  174 us (54%)
  waiting for transfers between devices  101 us (31%)
  local copies, waits for them, and re-layouts  19.2 us (6%)
  matrix products  12.8 us (4%)
  other arithmetic  8.22 us (3%)
  starting transfers between devices  6.62 us (2%)
    all_to_all x1, blocking collectives, shards(): lax.all_to_all(copies, 'ctx', split_axis=0, concat_axis=0, tiled=True)  99.7 us
    all_to_all x1, waiting for transfers between devices, shards(): lax.all_to_all(partial_out.reshape(sources, item_count, width_model), 'ct...  92.2 us
    all_gather x1, blocking collectives, shards(): lax.all_gather(key_states, 'ctx', axis=1, tiled=True)  29.6 us
    all_gather x1, blocking collectives, shards(): lax.all_gather(value_states, 'ctx', axis=1, tiled=True)  27.8 us
    all_to_all x1, blocking collectives, shards(): lax.all_to_all(outgoing, 'exp', split_axis=1, concat_axis=1, tiled=True)  17.1 us
    ppermute x3, waiting for transfers between devices, shards(): lax.ppermute(sent, 'exp', [(i, (i + step) % length) for i in range(length)])  8.52 us
    dot_general x1, matrix products, shards(): jnp.dot(active, down_piece, preferred_element_type=jnp.float32)  7.05 us
  transfers between devices with their start and end apart: 4, of which 3 were waited for; matrix products, arithmetic and copies ran while one was open for 1% of the time, Pallas kernels for 0%

profile of v1, /device:TPU:0, one launch (start us, length us, event | category | flops | bytes accessed | tf_op | source)
XLA Modules:
  0.0 322.4 jit_solution(9100023066045422515)
XLA Ops:
  0.0 1.2 slice_bitcast_fusion
  1.4 29.6 %all_gather.6 = bf16[1,1024,256]{1,2,0:T(8,128)(2,1)S(1)} all-gather(bf16[1,128,256]{1,2,0:T(8,128)(2,1)S(1)} %copy.28), channel_id=1, replica_groups=mesh['ctx'=8,'exp'=4] {'ctx'}, dimensions={1}, use_global_device_ids=true | all-gather | bytes 589824 | tf_op jit(solution)/shard_map/all_gather | solution.py:151
  31.1 27.8 %all_gather.7 = bf16[1,1024,256]{1,2,0:T(8,128)(2,1)S(1)} all-gather(bf16[1,128,256]{1,2,0:T(8,128)(2,1)S(1)} %copy.29), channel_id=1, replica_groups=mesh['ctx'=8,'exp'=4] {'ctx'}, dimensions={1}, use_global_device_ids=true | all-gather | bytes 589824 | tf_op jit(solution)/shard_map/all_gather | solution.py:152
  59.0 0.8 broadcast_in_dim.78
  59.8 0.8 broadcast_in_dim.78.clone
  60.7 9.5 %while.24 = (s32[]{:T(128)}, f32[2,512]{1,0:T(2,128)S(1)}, f32[2,512]{1,0:T(2,128)S(1)}, f32[2,512,128]{2,1,0:T(8,128)}, f32[2,512]{1,0:T(2,128)S(1)}, /*index=5...) while((s32[]{:T(128)}, f32[2,512]{1,0:T(2,128)S(1)}, ...), condition=%wide.region_9.10_spmd.clone, body=%wide.region_0.9_spmd.clone.sunk | while | flops 551557120 | bytes 29000316 | solution.py:95
  61.1 3.4 %conditional.7 = ((f32[2,512]{1,0:T(2,128)S(1)}, f32[2,512]{1,0:T(2,128)S(1)}, f32[2,512,128]{2,1,0:T(8,128)})) conditional(s32[]{:T(128)} %convert_element_type.131, (f32[2,512]{1,0:T(2,128)S(1)}, f32[2,512]{1,0:T(2,128)S(1)}, f32[2,512,128]{2,1,0:T(8,128)}) %tuple.68, (s32[]{:T(128)}, s32[]{:T(128)}, bf16[2,512,128]{2,1,0:T(8,128)(2,1)S(1)}, ...), branch_computations={%region_5.5_spmd, %region_6.8_spmd} | conditional | flops 275778560 | bytes 13449312 | solution.py:92
  62.6 1.1 convolution_add_fusion.1
  63.7 0.8 copy-done.6
  64.5 2.6 conditional.6
  66.0 1.1 convolution_add_fusion
  68.4 1.0 copy-done.3
  69.4 0.8 copy-done.4
  70.2 1.3 fusion.39
  73.5 1.0 scatter_custom_fusion
  74.5 2.3 gather_fusion
  76.9 1.3 copy.36
  78.2 17.1 %all_to_all.15 = bf16[2,4,32,2048]{3,2,0,1:T(8,128)(2,1)S(1)} all-to-all(bf16[2,4,32,2048]{3,2,0,1:T(8,128)(2,1)S(1)} %copy.36), channel_id=1, replica_groups=mesh['ctx'=8,'exp'=4] {'exp'}, dimensions={1} | all-to-all | bytes 2097152 | tf_op jit(solution)/shard_map/all_to_all | solution.py:184
  95.8 99.7 %all_to_all.16 = bf16[8,128,2048]{2,1,0:T(8,128)(2,1)S(1)} all-to-all(bf16[8,128,2048]{2,1,0:T(8,128)(2,1)S(1)} %bitcast.103), channel_id=1, replica_groups=mesh['ctx'=8,'exp'=4] {'ctx'}, dimensions={0} | all-to-all | bytes 8388608 | tf_op jit(solution)/shard_map/all_to_all | solution.py:191
  195.6 2.0 copy-done.2
  197.6 2.5 fusion.30
  200.0 7.1 %convolution_convert_fusion = bf16[1024,2048]{1,0:T(8,128)(2,1)} fusion(bf16[1024,2048]{1,0:T(8,128)(2,1)} %bitcast.109, bf16[1,1,192,2048]{3,2,1,0:T(8,128)(2,1)S(1)} %copy-done, bf16[1,1,192,2048]{3,2,1,0:T(8,128)(2,1)S(1)} %copy-done.13, f32[1024,192]{0,1:T(8,128)} %fusion.30), kind=kOutput, calls=%fused_computation.43 | convolution fusion | flops 1613889536 | bytes 10747904 | tf_op jit(solution)/shard_map/dot_general | solution.py:198
  207.1 4.6 %all-to-all-start.2 = ((bf16[8,128,2048]{2,1,0:T(8,128)(2,1)}), bf16[8,128,2048]{2,1,0:T(8,128)(2,1)}, u32[]{:S(2)}, u32[]{:S(2)}) async-start(bf16[8,128,2048]{2,1,0:T(8,128)(2,1)} %bitcast.107), calls=%async_computation.2 | async-start | bytes 8388608 | tf_op jit(solution)/shard_map/all_to_all | solution.py:201
  211.7 92.2 %all-to-all-done.2 = bf16[8,128,2048]{2,1,0:T(8,128)(2,1)} async-done(((bf16[8,128,2048]{2,1,0:T(8,128)(2,1)}), bf16[8,128,2048]{2,1,0:T(8,128)(2,1)}, u32[]{:S(2)}, u32[]{:S(2)}) %all-to-all-start.2) | async-done | bytes 4194336 | tf_op jit(solution)/shard_map/all_to_all | solution.py:201
  304.0 3.1 reduce_sum.57
  308.4 1.4 collective-permute-start.2
  309.8 6.6 %collective-permute-done = bf16[1,2,1,32,2048]{4,3,0,1,2:T(8,128)(2,1)} collective-permute-done((bf16[1,2,1,32,2048]{4,3,0,1,2:T(8,128)(2,1)}, bf16[1,2,1,32,2048]{4,3,0,1,2:T(8,128)(2,1)}, u32[]{:S(2)}, u32[]{:S(2)}) %collective-permute-start) | collective-permute-done | bytes 262176 | tf_op jit(solution)/shard_map/ppermute | solution.py:220
  316.4 1.0 constant_dynamic-update-slice_fusion.1
  317.4 1.0 constant_dynamic-update-slice_fusion
  318.4 2.0 collective-permute-done.2
  320.4 0.9 gather_fusion.1
  321.3 1.1 fusion.37
  (92 shorter events, 8.9 us)
Async XLA Ops:
  0.0 200.0 %copy-start = (bf16[1,1,192,2048]{3,2,1,0:T(8,128)(2,1)S(1)}, bf16[1,1,192,2048]{3,2,1,0:T(8,128)(2,1)}, u32[]{:S(2)}) copy-start(bf16[1,1,192,2048]{3,2,1,0:T(8,128)(2,1)} %param.23) | copy-start | bytes 2359300
  0.0 1.3 copy-start.8
  0.0 31.0 %copy-start.9 = (bf16[1,128,256]{2,1,0:T(8,128)(2,1)S(1)}, bf16[1,128,256]{2,1,0:T(8,128)(2,1)}, u32[]{:S(2)}) copy-start(bf16[1,128,256]{2,1,0:T(8,128)(2,1)} %param.18) | copy-start | bytes 196612
  61.1 3.4 %copy-start.3 = (f32[2,512,128]{2,1,0:T(8,128)S(1)}, f32[2,512,128]{2,1,0:T(8,128)}, u32[]{:S(2)}) copy-start(f32[2,512,128]{2,1,0:T(8,128)} %get-tuple-element.601) | copy-start | bytes 1572868 | tf_op jit(solution)/shard_map/while
  61.5 1.2 copy-start.5
  63.7 0.8 copy-start.6
  67.1 0.8 copy-start.4
  68.4 1.0 copy-start.3
  69.4 0.8 copy-start.4
  70.2 1.5 copy-start.7
  71.5 1.0 copy-start.1
  71.9 1.1 copy-start.10
  95.8 101.7 %copy-start.12 = (bf16[1,1,192,2048]{3,2,1,0:T(8,128)(2,1)S(1)}, bf16[1,1,192,2048]{3,2,1,0:T(8,128)(2,1)}, u32[]{:S(2)}) copy-start(bf16[1,1,192,2048]{3,2,1,0:T(8,128)(2,1)} %param.21) | copy-start | bytes 2359300
  195.6 2.0 copy-start.2
  197.6 2.5 copy-start.13
  207.1 96.9 %all-to-all-start.2 = ((bf16[8,128,2048]{2,1,0:T(8,128)(2,1)}), bf16[8,128,2048]{2,1,0:T(8,128)(2,1)}, u32[]{:S(2)}, u32[]{:S(2)}) async-start(bf16[8,128,2048]{2,1,0:T(8,128)(2,1)} %bitcast.107), calls=%async_computation.2 | async-start | bytes 8388608 | tf_op jit(solution)/shard_map/all_to_all | solution.py:201
  307.8 8.6 %collective-permute-start = (bf16[1,2,1,32,2048]{4,3,0,1,2:T(8,128)(2,1)}, bf16[1,2,1,32,2048]{4,3,0,1,2:T(8,128)(2,1)}, u32[]{:S(2)}, u32[]{:S(2)}) collective-permute-start(bf16[1,2,1,32,2048]{4,3,0,1,2:T(8,128)(2,1)} %get-tuple-element.455), channel_id=1, source_target_pairs={{0,1},{1,2},{2,3},{3,0},{4,5},{5,6},{6,7},{7,4},{8,9},{9,10},{10,1... | collective-permute-start | bytes 786440 | tf_op jit(solution)/shard_map/ppermute | solution.py:220
  307.8 9.6 %collective-permute-start.1 = (bf16[1,2,1,32,2048]{4,3,0,1,2:T(8,128)(2,1)S(1)}, bf16[1,2,1,32,2048]{4,3,0,1,2:T(8,128)(2,1)}, u32[]{:S(2)}, u32[]{:S(2)}) collective-permute-start(bf16[1,2,1,32,2048]{4,3,0,1,2:T(8,128)(2,1)S(1)} %get-tuple-element.454), channel_id=1, source_target_pairs={{0,2},{1,3},{2,0},{3,1},{4,6},{5,7},{6,4},{7,5},{8,10},{9,11},{10,... | collective-permute-start | bytes 786440 | tf_op jit(solution)/shard_map/ppermute | solution.py:220
  308.4 11.9 %collective-permute-start.2 = (bf16[1,2,1,32,2048]{4,3,0,1,2:T(8,128)(2,1)S(1)}, bf16[1,2,1,32,2048]{4,3,0,1,2:T(8,128)(2,1)S(1)}, u32[]{:S(2)}, u32[]{:S(2)}) collective-permute-start(bf16[1,2,1,32,2048]{4,3,0,1,2:T(8,128)(2,1)S(1)} %get-tuple-element.453), channel_id=1, source_target_pairs={{0,3},{1,0},{2,1},{3,2},{4,7},{5,4},{6,5},{7,6},{8,11},{9,8},{10,9... | collective-permute-start | bytes 786440 | tf_op jit(solution)/shard_map/ppermute | solution.py:220
  320.4 1.0 copy-start.11
